TPU v7x, 256 devices: a whole 4x4x8 slice. The times are simulated.
256 devices in a mesh: prow: 16 (over x, y), pcol: 16 (over z, core).
Axes of the slice: x: 4, y: 4, z: 8, core: 2. Of those that a mesh axis runs over, the one named last changes fastest.
Arguments:
- left_factor: bfloat16 [64, 32, 2048, 128], P('prow', 'pcol'), may hold values from -0.8984375 to 0.8984375
- right_factor: bfloat16 [64, 32, 2048, 128], P('prow', 'pcol'), may hold values from -0.8984375 to 0.8984375
- pivot_left: bfloat16 [32, 2048, 128], P('pcol', 'prow'), may hold values from -0.8984375 to 0.8984375
- pivot_right: bfloat16 [32, 2048, 128], P('pcol', 'prow'), may hold values from -0.8984375 to 0.8984375
- target_left: bfloat16 [2048, 64, 128], P('pcol', 'prow'), may hold values from -6 to 6
- target_right: bfloat16 [2048, 64, 128], P('pcol', 'prow'), may hold values from -6 to 6
- probe: bfloat16 [2048, 128], P('prow'), may hold values from -6 to 6
- ranks: int32 [64, 32], P('prow', 'pcol'), may hold values from 16 to 128
Outputs:
- basis: float32 [2048, 64, 128], P('pcol', 'prow')
- coefficient: float32 [2048, 64, 128], P('pcol', 'prow')
All inputs are finite; a program needn't handle non-finite values.
Results may differ from a plain program's by a relative error of at most 0.0038.
Values may be sent and summed in bfloat16 or wider, within the bound.
No kernel may reach another device: no remote copies, remote signals or barrier semaphores. Data moves between devices by JAX's collectives and lax.ppermute only.
A program may use at most 64 MiB of HBM per device.

v0:
```python
import jax
import jax.numpy as jnp
from jax import lax
from jax.sharding import PartitionSpec as P

exact_mode = lax.Precision.HIGHEST


def solve_rows(lower_factor, samples):
    stacked = jnp.transpose(samples, (1, 0, 2))
    solved = lax.linalg.triangular_solve(
        lower_factor, stacked, left_side=False, lower=True, transpose_a=True
    )
    return jnp.transpose(solved, (1, 0, 2))


def per_device(
    left_factor, right_factor, pivot_left, pivot_right, target_left, target_right, probe, ranks
):
    pivot_whole, pivot_other, probe_whole = (
        lax.all_gather(pivot_left, "prow", axis=1, tiled=True),
        lax.all_gather(pivot_right, "prow", axis=1, tiled=True),
        lax.all_gather(probe, "prow", axis=0, tiled=True),
    )
    order_full = left_factor.shape[2]
    rank_span = left_factor.shape[3]
    row_count = target_left.shape[0]
    first_row = lax.axis_index("pcol") * row_count
    probe_slice = lax.dynamic_slice_in_dim(probe_whole, first_row, row_count, 0)
    sample_part = jnp.einsum(
        "bir,bs->irs", target_right, probe_slice, preferred_element_type=jnp.float32
    )
    target_sample = lax.psum(sample_part, "pcol")
    pivot_sample = jnp.einsum(
        "jbr,bs->jrs", pivot_whole, probe_whole, preferred_element_type=jnp.float32
    )
    rank_index = lax.broadcasted_iota(jnp.int32, ranks.shape + (rank_span,), 2)
    rank_mask = (rank_index < ranks[:, :, None]).astype(jnp.float32)
    coupling = jnp.einsum(
        "ijbr,jbs->ijrs", right_factor, pivot_other, preferred_element_type=jnp.float32
    )
    coupling = coupling * rank_mask[:, :, :, None]
    weights = jnp.einsum("ijrs,jst->ijrt", coupling, pivot_sample, precision=exact_mode).astype(
        jnp.bfloat16
    )
    target_term = jnp.einsum(
        "bis,ist->bit", target_left.astype(jnp.float32), target_sample, precision=exact_mode
    )
    samples_own = (
        lax.psum_scatter(
            -jnp.einsum("ijbr,ijrt->bit", left_factor, weights, preferred_element_type=jnp.float32),
            "pcol",
            scatter_dimension=0,
            tiled=True,
        )
        + target_term
    )
    gram_part = jnp.einsum("bir,bis->irs", samples_own, samples_own, precision=exact_mode)
    gram_matrix = lax.psum(gram_part, "pcol") / order_full
    lower_factor = jnp.linalg.cholesky(gram_matrix)
    basis_rows = solve_rows(lower_factor, samples_own)
    basis_full = lax.all_gather(basis_rows.astype(jnp.bfloat16), "pcol", axis=0, tiled=True)
    basis_half = basis_rows.astype(jnp.bfloat16)
    correlation = jnp.einsum(
        "ijbr,bit->ijrt", left_factor, basis_full, preferred_element_type=jnp.float32
    )
    reduced = jnp.einsum("ijrs,ijrt->ijst", coupling, correlation, precision=exact_mode).astype(
        jnp.bfloat16
    )
    correlation_part = jnp.einsum(
        "bis,bit->ist", target_left, basis_half, preferred_element_type=jnp.float32
    )
    target_correlation = lax.psum(correlation_part, "pcol").astype(jnp.bfloat16)
    projected = lax.psum_scatter(
        -jnp.einsum("jbs,ijst->bit", pivot_whole, reduced, preferred_element_type=jnp.float32),
        "pcol",
        scatter_dimension=0,
        tiled=True,
    )
    own_term = jnp.einsum(
        "bis,ist->bit", target_right, target_correlation, preferred_element_type=jnp.float32
    )
    coefficient = (projected + own_term) / order_full
    return (basis_rows, coefficient)


def solution(mesh):
    in_specs = (
        P("prow", "pcol", None, None),
        P("prow", "pcol", None, None),
        P("pcol", "prow", None),
        P("pcol", "prow", None),
        P("pcol", "prow", None),
        P("pcol", "prow", None),
        P("prow", None),
        P("prow", "pcol"),
    )
    out_specs = (P("pcol", "prow", None), P("pcol", "prow", None))
    return jax.shard_map(
        per_device, mesh=mesh, in_specs=in_specs, out_specs=out_specs, check_vma=False
    )
```

profile of v0, /device:TPU:6, one launch (start us, length us, event | category | flops | bytes accessed | tf_op | source)
XLA Modules:
  0.0 534.8 jit_solution(9930926881617621154)
XLA Ops:
  8.8 1.6 copy.21
  10.4 24.0 %all_gather.13 = bf16[2048,128]{1,0:T(8,128)(2,1)S(1)} all-gather(bf16[128,128]{1,0:T(8,128)(2,1)} %param.14), channel_id=1, replica_groups=mesh['prow'=16,'pcol'=16] {'prow'}, dimensions={0}, use_global_device_ids=true | all-gather | bytes 557056 | tf_op jit(solution)/shard_map/all_gather | solution.py:23
  34.4 1.8 convolution_bitcast_fusion.4
  37.1 24.4 %all-gather.4.cloned.1.call-done = bf16[2,2048,128]{2,1,0:T(8,128)(2,1)} async-done(((bf16[2,128,128]{2,1,0:T(8,128)(2,1)}), bf16[2,2048,128]{2,1,0:T(8,128)(2,1)}) %all-gather.4.cloned.1.call-update) | async-done | bytes 1048592 | tf_op jit(solution)/shard_map/all_gather | solution.py:21
  61.4 1.7 convolution_bitcast_fusion.5
  63.1 48.8 %all-gather.6.cloned.1.call-done = bf16[2,2048,128]{1,2,0:T(8,128)(2,1)} async-done(((bf16[2,128,128]{1,2,0:T(8,128)(2,1)}), bf16[2,2048,128]{1,2,0:T(8,128)(2,1)}) %all-gather.6.cloned.1.call-update) | async-done | bytes 1048592 | tf_op jit(solution)/shard_map/all_gather | solution.py:22
  112.0 3.4 fusion.9
  116.0 3.4 fusion.1
  119.5 27.8 %all-reduce.4.cloned.1.call-done = f32[4,128,128]{1,2,0:T(8,128)} async-done(((f32[4,128,128]{1,2,0:T(8,128)}), f32[4,128,128]{1,2,0:T(8,128)}) %all-reduce.4.cloned.1.call-update) | async-done | bytes 262160 | tf_op jit(solution)/shard_map/psum | solution.py:33
  147.4 66.3 %reduce-scatter.3.cloned.1.call-done = f32[128,4,128]{0,2,1:T(8,128)} async-done(((f32[2048,4,128]{0,2,1:T(8,128)}), f32[128,4,128]{0,2,1:T(8,128)}) %reduce-scatter.3.cloned.1.call-update) | async-done | bytes 262160 | tf_op jit(solution)/shard_map/reduce_scatter | solution.py:50
  213.6 1.4 fusion.13
  215.1 1.4 fusion.35
  216.6 107.9 %all-reduce.6.cloned.1.call-done = f32[4,128,128]{1,2,0:T(8,128)} async-done(((f32[4,128,128]{1,2,0:T(8,128)}), f32[4,128,128]{1,2,0:T(8,128)}) %all-reduce.6.cloned.1.call-update) | async-done | bytes 262160 | tf_op jit(solution)/shard_map/psum | solution.py:59
  325.6 1.0 fusion.23
  326.6 46.9 %custom-call.7 = f32[4,128,128]{2,1,0:T(8,128)S(1)} custom-call(f32[4,128,128]{2,1,0:T(8,128)S(1)} %fusion.23), custom_call_target="Cholesky" | custom-call | tf_op jit(solution)/shard_map/jit(cholesky)/cholesky | solution.py:60
  373.8 39.3 %custom-call.8 = f32[4,1,128,128]{2,3,1,0:T(8,128)S(1)} custom-call(f32[4,1,128,128]{3,2,1,0:T(8,128)S(1)} %select_bitcast_fusion), custom_call_target="InvertDiagBlocksLowerTriangular" | custom-call | tf_op jit(solution)/shard_map/triangular_solve | solution.py:11
  413.1 1.3 fusion.34
  414.6 40.2 %all-gather.8.cloned.1.call-done = bf16[2048,4,128]{2,0,1:T(8,128)(2,1)} async-done(((bf16[128,4,128]{2,0,1:T(8,128)(2,1)}), bf16[2048,4,128]{2,0,1:T(8,128)(2,1)}) %all-gather.8.cloned.1.call-update) | async-done | bytes 2097168 | tf_op jit(solution)/shard_map/all_gather | solution.py:62
  454.8 3.8 fusion.4
  458.9 1.2 convolution_convert_fusion.1
  460.2 2.7 fusion
  464.0 49.8 %all-reduce.7 = bf16[4,128,128]{1,2,0:T(8,128)(2,1)S(1)} all-reduce(f32[4,128,128]{1,2,0:T(8,128)S(1)} %convolution_bitcast_fusion.3), channel_id=1, replica_groups=mesh['prow'=16,'pcol'=16] {'pcol'}, use_global_device_ids=true, to_apply=%region_6.7 | all-reduce | flops 65536 | bytes 393216 | tf_op jit(solution)/shard_map/psum | solution.py:73
  513.8 11.4 %reduce-scatter.5.cloned.1.call-done = f32[128,4,128]{0,2,1:T(8,128)} async-done(((f32[2048,4,128]{0,2,1:T(8,128)}), f32[128,4,128]{0,2,1:T(8,128)}) %reduce-scatter.5.cloned.1.call-update) | async-done | bytes 262160 | tf_op jit(solution)/shard_map/reduce_scatter | solution.py:74
  525.2 1.2 fusion.15
  (37 shorter events, 6.4 us)
Async XLA Ops:
  8.0 205.7 %copy-start = (bf16[128,4,128]{2,1,0:T(4,128)(2,1)S(1)}, bf16[128,4,128]{2,1,0:T(4,128)(2,1)}, u32[]{:S(2)}) copy-start(bf16[128,4,128]{2,1,0:T(4,128)(2,1)} %param.12) | copy-start | bytes 393220
  8.0 53.4 %all-gather.4.cloned.1.call-start = ((), (), s32[]{:S(2)}) async-start(), calls=%async_computation.2 | async-start | bytes 1114112 | tf_op jit(solution)/shard_map/all_gather | solution.py:21
  8.7 103.2 %all-gather.6.cloned.1.call-start = ((), (), s32[]{:S(2)}) async-start(), calls=%async_computation.3 | async-start | bytes 1114112 | tf_op jit(solution)/shard_map/all_gather | solution.py:22
  10.4 137.0 %all-reduce.4.cloned.1.call-start = ((), (), s32[]{:S(2)}) async-start(), calls=%async_computation.5 | async-start | bytes 524288 | tf_op jit(solution)/shard_map/psum | solution.py:33
  36.2 177.4 %reduce-scatter.3.cloned.1.call-start = ((), (), s32[]{:S(2)}) async-start(), calls=%async_computation.4 | async-start | bytes 4456448 | tf_op jit(solution)/shard_map/reduce_scatter | solution.py:50
  112.0 4.0 copy-start.1
  119.5 205.0 %all-reduce.6.cloned.1.call-start = ((), (), s32[]{:S(2)}) async-start(), calls=%async_computation.6 | async-start | bytes 524288 | tf_op jit(solution)/shard_map/psum | solution.py:59
  216.5 238.3 %all-gather.8.cloned.1.call-start = ((), (), s32[]{:S(2)}) async-start(), calls=%async_computation.7 | async-start | bytes 2228224 | tf_op jit(solution)/shard_map/all_gather | solution.py:62
  414.4 45.8 %copy-start.2 = (bf16[2,2048,128]{2,1,0:T(8,128)(2,1)S(1)}, bf16[2,2048,128]{2,1,0:T(8,128)(2,1)}, u32[]{:S(2)}) copy-start(bf16[2,2048,128]{2,1,0:T(8,128)(2,1)} %all-gather.4.cloned.1.call-done) | copy-start | bytes 3145732
  414.4 110.8 %reduce-scatter.5.cloned.1.call-start = ((), (), s32[]{:S(2)}) async-start(), calls=%async_computation.8 | async-start | bytes 4456448 | tf_op jit(solution)/shard_map/reduce_scatter | solution.py:74
  460.2 2.7 copy-start.3
  462.9 62.3 %copy-start.4 = (bf16[128,4,128]{2,1,0:T(4,128)(2,1)S(1)}, bf16[128,4,128]{2,1,0:T(4,128)(2,1)}, u32[]{:S(2)}) copy-start(bf16[128,4,128]{2,1,0:T(4,128)(2,1)} %param.13) | copy-start | bytes 393220
Sparse Core Ops, SparseCore 0:
  11.3 50.0 all-gather.3
  64.4 47.5 all-gather.5
Sparse Core Ops, SparseCore 1:
  36.3 111.0 all-reduce.3
  149.8 63.8 reduce-scatter.2
  216.5 107.9 all-reduce.5
  414.4 40.3 all-gather.7
  463.0 62.1 reduce-scatter.4
where the time goes:
time: 535 us
  waiting for transfers between devices  328 us (61%)
  other arithmetic  89.2 us (17%)
  blocking collectives  73.7 us (14%)
  matrix products  24.1 us (5%)
  between operations  15.9 us (3%)
    psum x1, waiting for transfers between devices, per_device(): gram_matrix = lax.psum(gram_part, 'pcol') / order_full  108 us
    reduce_scatter x1, waiting for transfers between devices, per_device(): lax.psum_scatter(-jnp.einsum('ijbr,ijrt->bit', left_factor, weights, pref...  66.3 us
    psum x1, blocking collectives, per_device(): target_correlation = lax.psum(correlation_part, 'pcol').astype(jnp.bfloat16)  49.8 us
    all_gather x1, waiting for transfers between devices, per_device(): lax.all_gather(pivot_right, 'prow', axis=1, tiled=True)  48.8 us
    another operation x4, other arithmetic, per_device(): lower_factor = jnp.linalg.cholesky(gram_matrix)  47.1 us
    all_gather x1, waiting for transfers between devices, per_device(): lax.all_gather(basis_rows.astype(jnp.bfloat16), 'pcol', axis=0, tiled=True)  40.2 us
    another operation x3, other arithmetic, solve_rows(): lax.linalg.triangular_solve(lower_factor, stacked, left_side=False, lower...  39.4 us
    psum x1, waiting for transfers between devices, per_device(): target_sample = lax.psum(sample_part, 'pcol')  27.8 us
  transfers between devices with their start and end apart: 7, of which 7 were waited for; matrix products, arithmetic and copies ran while one was open for 3% of the time, Pallas kernels for 0%

commit v1 on v0

--- a/solution.py
+++ b/solution.py
@@ -4,6 +4,12 @@
 from jax.sharding import PartitionSpec as P
 
 exact_mode = lax.Precision.HIGHEST
+
+
+def add_all(shard, name):
+    pieces = lax.all_gather(shard, name, axis=0, tiled=False)
+    summed = pieces.sum(axis=0)
+    return summed
 
 
 def solve_rows(lower_factor, samples):
@@ -70,7 +76,7 @@
     correlation_part = jnp.einsum(
         "bis,bit->ist", target_left, basis_half, preferred_element_type=jnp.float32
     )
-    target_correlation = lax.psum(correlation_part, "pcol").astype(jnp.bfloat16)
+    target_correlation = add_all(correlation_part, "pcol").astype(jnp.bfloat16)
     projected = lax.psum_scatter(
         -jnp.einsum("jbs,ijst->bit", pivot_whole, reduced, preferred_element_type=jnp.float32),
         "pcol",

time: 535 us -> 573 us (1.071)
  waiting for transfers between devices: 328 us -> 410 us
  blocking collectives: 73.7 us -> 24.1 us
    reduce_scatter x1, waiting for transfers between devices: 11.4 us -> 61.8 us  [per_device(): lax.psum_scatter(-jnp.einsum('jbs,ijst->bit', pivot_whole, reduced, prefe...]
    psum x1 -> x0, blocking collectives: 49.8 us -> none  [per_device(): target_correlation = lax.psum(correlation_part, 'pcol').astype(jnp.bfloat16)]
    all_gather x0 -> x1, waiting for transfers between devices: none -> 34.4 us  [add_all(): pieces = lax.all_gather(shard, name, axis=0, tiled=False)]
  transfers between devices with their start and end apart: 7 -> 8, of which waited for: 7 -> 8; matrix products, arithmetic and copies ran while one was open for 3% -> 5% of each run, Pallas kernels for 0% -> 0%
where the time goes in v1:
time: 573 us; the launch traced here: 572 us
  waiting for transfers between devices  410 us (72%)
  other arithmetic  91.6 us (16%)
  matrix products  25 us (4%)
  blocking collectives  24.1 us (4%)
  between operations  15.7 us (3%)
  local copies, waits for them, and re-layouts  5.87 us (1%)
    psum x1, waiting for transfers between devices, per_device(): gram_matrix = lax.psum(gram_part, 'pcol') / order_full  108 us
    reduce_scatter x1, waiting for transfers between devices, per_device(): lax.psum_scatter(-jnp.einsum('ijbr,ijrt->bit', left_factor, weights, pref...  66.3 us
    reduce_scatter x1, waiting for transfers between devices, per_device(): lax.psum_scatter(-jnp.einsum('jbs,ijst->bit', pivot_whole, reduced, prefe...  61.8 us
    all_gather x1, waiting for transfers between devices, per_device(): lax.all_gather(pivot_right, 'prow', axis=1, tiled=True)  48.3 us
    another operation x4, other arithmetic, per_device(): lower_factor = jnp.linalg.cholesky(gram_matrix)  47.1 us
    another operation x3, other arithmetic, solve_rows(): lax.linalg.triangular_solve(lower_factor, stacked, left_side=False, lower...  39.4 us
    all_gather x1, waiting for transfers between devices, per_device(): lax.all_gather(basis_rows.astype(jnp.bfloat16), 'pcol', axis=0, tiled=True)  38.1 us
    all_gather x1, waiting for transfers between devices, add_all(): pieces = lax.all_gather(shard, name, axis=0, tiled=False)  34.4 us
  transfers between devices with their start and end apart: 8, of which 8 were waited for; matrix products, arithmetic and copies ran while one was open for 5% of the time, Pallas kernels for 0%

profile of v1, /device:TPU:6, one launch (start us, length us, event | category | flops | bytes accessed | tf_op | source)
XLA Modules:
  0.0 572.5 jit_solution(2333357237123412623)
XLA Ops:
  8.1 1.6 copy.62
  9.7 1.6 copy.63
  11.4 24.1 %all_gather.19 = bf16[2048,128]{1,0:T(8,128)(2,1)S(1)} all-gather(bf16[128,128]{1,0:T(8,128)(2,1)} %param.14), channel_id=1, replica_groups=mesh['prow'=16,'pcol'=16] {'prow'}, dimensions={0}, use_global_device_ids=true | all-gather | bytes 557056 | tf_op jit(solution)/shard_map/all_gather | solution.py:29
  35.5 1.8 convolution_bitcast_fusion.4
  38.2 24.5 %all-gather.6.cloned.1.call-done = bf16[2,2048,128]{1,2,0:T(8,128)(2,1)} async-done(((bf16[2,128,128]{1,2,0:T(8,128)(2,1)}), bf16[2,2048,128]{1,2,0:T(8,128)(2,1)}) %all-gather.6.cloned.1.call-update) | async-done | bytes 1048592 | tf_op jit(solution)/shard_map/all_gather | solution.py:27
  62.7 1.7 convolution_bitcast_fusion.5
  64.4 48.3 %all-gather.8.cloned.1.call-done = bf16[2,2048,128]{1,2,0:T(8,128)(2,1)} async-done(((bf16[2,128,128]{1,2,0:T(8,128)(2,1)}), bf16[2,2048,128]{1,2,0:T(8,128)(2,1)}) %all-gather.8.cloned.1.call-update) | async-done | bytes 1048592 | tf_op jit(solution)/shard_map/all_gather | solution.py:28
  112.7 3.4 fusion.12
  116.7 3.4 fusion.1
  120.2 28.2 %all-reduce.3.cloned.1.call-done = f32[4,128,128]{1,2,0:T(8,128)} async-done(((f32[4,128,128]{1,2,0:T(8,128)}), f32[4,128,128]{1,2,0:T(8,128)}) %all-reduce.3.cloned.1.call-update) | async-done | bytes 262160 | tf_op jit(solution)/shard_map/psum | solution.py:39
  148.4 66.3 %reduce-scatter.3.cloned.1.call-done = f32[128,4,128]{0,2,1:T(8,128)} async-done(((f32[2048,4,128]{0,2,1:T(8,128)}), f32[128,4,128]{0,2,1:T(8,128)}) %reduce-scatter.3.cloned.1.call-update) | async-done | bytes 262160 | tf_op jit(solution)/shard_map/reduce_scatter | solution.py:56
  214.7 1.4 fusion.16
  216.1 1.4 fusion.37
  217.6 107.9 %all-reduce.5.cloned.1.call-done = f32[4,128,128]{1,2,0:T(8,128)} async-done(((f32[4,128,128]{1,2,0:T(8,128)}), f32[4,128,128]{1,2,0:T(8,128)}) %all-reduce.5.cloned.1.call-update) | async-done | bytes 262160 | tf_op jit(solution)/shard_map/psum | solution.py:65
  327.6 46.9 %custom-call.7 = f32[4,128,128]{2,1,0:T(8,128)S(1)} custom-call(f32[4,128,128]{2,1,0:T(8,128)S(1)} %fusion.25), custom_call_target="Cholesky" | custom-call | tf_op jit(solution)/shard_map/jit(cholesky)/cholesky | solution.py:66
  374.8 39.3 %custom-call.8 = f32[4,1,128,128]{2,3,1,0:T(8,128)S(1)} custom-call(f32[4,1,128,128]{3,2,1,0:T(8,128)S(1)} %select_bitcast_fusion), custom_call_target="InvertDiagBlocksLowerTriangular" | custom-call | tf_op jit(solution)/shard_map/triangular_solve | solution.py:17
  414.1 1.3 fusion.36
  417.7 38.1 %all-gather.10.cloned.1.call-done = bf16[2048,4,128]{2,0,1:T(8,128)(2,1)} async-done(((bf16[128,4,128]{2,0,1:T(8,128)(2,1)}), bf16[2048,4,128]{2,0,1:T(8,128)(2,1)}) %all-gather.10.cloned.1.call-update) | async-done | bytes 2097168 | tf_op jit(solution)/shard_map/all_gather | solution.py:68
  455.8 3.8 fusion.6
  459.5 1.2 convolution_convert_fusion.1
  460.8 2.7 fusion
  464.4 34.4 %all-gather.12.cloned.1.call-done = f32[64,128,128]{2,1,0:T(8,128)} async-done(((f32[4,128,128]{2,1,0:T(8,128)}), f32[64,128,128]{2,1,0:T(8,128)}) %all-gather.12.cloned.1.call-update) | async-done | bytes 4194320 | tf_op jit(solution)/shard_map/all_gather | solution.py:10
  498.8 2.4 reduce_sum.9
  501.2 61.8 %reduce-scatter.5.cloned.1.call-done = f32[128,4,128]{0,2,1:T(8,128)} async-done(((f32[2048,4,128]{0,2,1:T(8,128)}), f32[128,4,128]{0,2,1:T(8,128)}) %reduce-scatter.5.cloned.1.call-update) | async-done | bytes 262160 | tf_op jit(solution)/shard_map/reduce_scatter | solution.py:80
  (39 shorter events, 9.3 us)
Async XLA Ops:
  8.0 206.7 %copy-start = (bf16[128,4,128]{2,1,0:T(4,128)(2,1)S(1)}, bf16[128,4,128]{2,1,0:T(4,128)(2,1)}, u32[]{:S(2)}) copy-start(bf16[128,4,128]{2,1,0:T(4,128)(2,1)} %param.12) | copy-start | bytes 393220
  8.0 54.7 %all-gather.6.cloned.1.call-start = ((), (), s32[]{:S(2)}) async-start(), calls=%async_computation.2 | async-start | bytes 1114112 | tf_op jit(solution)/shard_map/all_gather | solution.py:27
  9.7 103.0 %all-gather.8.cloned.1.call-start = ((), (), s32[]{:S(2)}) async-start(), calls=%async_computation.3 | async-start | bytes 1114112 | tf_op jit(solution)/shard_map/all_gather | solution.py:28
  11.3 137.1 %all-reduce.3.cloned.1.call-start = ((), (), s32[]{:S(2)}) async-start(), calls=%async_computation.5 | async-start | bytes 524288 | tf_op jit(solution)/shard_map/psum | solution.py:39
  37.4 177.3 %reduce-scatter.3.cloned.1.call-start = ((), (), s32[]{:S(2)}) async-start(), calls=%async_computation.4 | async-start | bytes 4456448 | tf_op jit(solution)/shard_map/reduce_scatter | solution.py:56
  112.7 4.0 copy-start.1
  120.1 205.4 %all-reduce.5.cloned.1.call-start = ((), (), s32[]{:S(2)}) async-start(), calls=%async_computation.6 | async-start | bytes 524288 | tf_op jit(solution)/shard_map/psum | solution.py:65
  217.5 238.3 %all-gather.10.cloned.1.call-start = ((), (), s32[]{:S(2)}) async-start(), calls=%async_computation.7 | async-start | bytes 2228224 | tf_op jit(solution)/shard_map/all_gather | solution.py:68
  415.4 83.4 %all-gather.12.cloned.1.call-start = ((), (), s32[]{:S(2)}) async-start(), calls=%async_computation.9 | async-start | bytes 4456448 | tf_op jit(solution)/shard_map/all_gather | solution.py:10
  417.4 43.4 %copy-start.2 = (bf16[2,2048,128]{1,2,0:T(8,128)(2,1)S(1)}, bf16[2,2048,128]{1,2,0:T(8,128)(2,1)}, u32[]{:S(2)}) copy-start(bf16[2,2048,128]{1,2,0:T(8,128)(2,1)} %all-gather.6.cloned.1.call-done) | copy-start | bytes 3145732
  417.4 145.6 %reduce-scatter.5.cloned.1.call-start = ((), (), s32[]{:S(2)}) async-start(), calls=%async_computation.8 | async-start | bytes 4456448 | tf_op jit(solution)/shard_map/reduce_scatter | solution.py:80
  463.5 99.5 %copy-start.3 = (bf16[128,4,128]{2,1,0:T(4,128)(2,1)S(1)}, bf16[128,4,128]{2,1,0:T(4,128)(2,1)}, u32[]{:S(2)}) copy-start(bf16[128,4,128]{2,1,0:T(4,128)(2,1)} %param.13) | copy-start | bytes 393220
Sparse Core Ops, SparseCore 0:
  11.8 50.8 all-gather.5
  65.1 47.5 all-gather.7
Sparse Core Ops, SparseCore 1:
  37.4 110.9 all-reduce.2
  150.8 63.8 reduce-scatter.2
  217.6 107.9 all-reduce.4
  415.5 40.3 all-gather.9
  458.2 40.5 all-gather.11
  501.3 61.6 reduce-scatter.4
